TPU v7x, 256 devices: a whole 4x4x8 slice. The times are simulated.
256 devices in a mesh: group: 8 (over z_hi, core), shard: 32 (over z_lo, y, x).
Axes of the slice: x: 4, y: 4, z: 8 (z_hi: 4, z_lo: 2; z = z_hi * 2 + z_lo), core: 2. Of those that a mesh axis runs over, the one named last changes fastest.
Arguments:
- latents: bfloat16 [512, 32, 32, 320], P(('group', 'shard')), may hold values from -6 to 6
- cotangent: bfloat16 [512, 32, 32, 320], P(('group', 'shard')), may hold values from -6 to 6
- weights: float32 [8, 2880, 320], P('group', 'shard'), may hold values from -0.109375 to 0.109375
- momentum: float32 [8, 2880, 320], P('group', 'shard'), may hold values from -6 to 6
- step: int32 [1], replicated, may hold values from 0 to 63
Outputs:
- activations: float32 [512, 32, 32, 320], P(('group', 'shard'))
- data_grad: float32 [512, 32, 32, 320], P(('group', 'shard'))
- new_weights: float32 [8, 2880, 320], P('group', 'shard')
- new_momentum: float32 [8, 2880, 320], P('group', 'shard')
Inputs may be any that keep to these rules, and one draw needn't show every extreme that they name: `step`: one value shared by all devices.
All inputs are finite; a program needn't handle non-finite values.
Results may differ from a plain program's by a relative error of at most 0.0029.
Values may be sent and summed in bfloat16 or wider, within the bound.
No kernel may reach another device: no remote copies, remote signals or barrier semaphores. Data moves between devices by JAX's collectives and lax.ppermute only.
A program may use at most 128 MiB of HBM per device.

v0:
```python
from functools import partial
import jax
import jax.numpy as jnp
from jax import lax
from jax.sharding import PartitionSpec as P

beta_rate = 0.9
peak_rate = 0.1
warm_steps = 64.0
tap_offsets = [(row_off, col_off) for row_off in (-1, 0, 1) for col_off in (-1, 0, 1)]


def from_partner(value, axis, bit):
    mask = 2**bit
    pairs = [(source, source ^ mask) for source in range(lax.axis_size(axis))]
    return lax.ppermute(value, axis, pairs)


def shifted_view(padded, row_off, col_off):
    height = padded.shape[1] - 2
    width = padded.shape[2] - 2
    return padded[:, 1 + row_off : 1 + row_off + height, 1 + col_off : 1 + col_off + width, :]


def conv_step(latents, cotangent, kernel):
    channels = kernel.shape[1]
    image_shape = latents.shape
    cell_count = image_shape[0] * image_shape[1] * image_shape[2]
    pad_in = jnp.pad(latents, ((0, 0), (1, 1), (1, 1), (0, 0)))
    pad_co = jnp.pad(cotangent, ((0, 0), (1, 1), (1, 1), (0, 0)))
    flat_co = cotangent.reshape(cell_count, channels)
    forward = jnp.zeros((cell_count, channels), jnp.float32)
    backward = jnp.zeros((cell_count, channels), jnp.float32)
    tap_grads = []
    for tap_index, (row_off, col_off) in enumerate(tap_offsets):
        tap_kernel = kernel[tap_index * channels : (tap_index + 1) * channels]
        moved_in = shifted_view(pad_in, row_off, col_off).reshape(cell_count, channels)
        moved_co = shifted_view(pad_co, -row_off, -col_off).reshape(cell_count, channels)
        forward = forward + jnp.dot(moved_in, tap_kernel, preferred_element_type=jnp.float32)
        backward = backward + lax.dot_general(
            moved_co, tap_kernel, (((1,), (1,)), ((), ())), preferred_element_type=jnp.float32
        )
        tap_grads.append(
            lax.dot_general(
                moved_in, flat_co, (((0,), (0,)), ((), ())), preferred_element_type=jnp.float32
            )
        )
    return (
        forward.reshape(image_shape),
        backward.reshape(image_shape),
        jnp.concatenate(tap_grads, 0),
    )


def trade_pair(payload, level):
    return from_partner(payload, "group", level)


def shards(latents, cotangent, weights, momentum, step):
    kernel_rows = weights[0].astype(jnp.bfloat16)
    kernel = lax.all_gather(kernel_rows, "shard", axis=0, tiled=True)
    forward, backward, partial_grad = conv_step(latents, cotangent, kernel)
    cells_group = lax.axis_size("shard") * latents.shape[0] * latents.shape[1] * latents.shape[2]
    grad_scale = float(cells_group) ** (-0.5)
    learn_rate = peak_rate * (step[0] + 1).astype(jnp.float32) / warm_steps
    shard_rows = weights.shape[1]
    summed = lax.psum(partial_grad, "shard")
    own_rows = lax.dynamic_slice_in_dim(summed, lax.axis_index("shard") * shard_rows, shard_rows, 0)
    moment_new = beta_rate * momentum[0] + own_rows * grad_scale
    updated = weights[0] - learn_rate * moment_new
    bit_count = lax.axis_size("group").bit_length() - 1
    branches = [partial(trade_pair, level=level_index) for level_index in range(bit_count)]
    partner_weights, partner_moment = lax.switch(
        step[0] % bit_count, branches, (updated, moment_new)
    )
    new_weights = (0.5 * (updated + partner_weights))[None]
    new_momentum = (0.5 * (moment_new + partner_moment))[None]
    return (forward, backward, new_weights, new_momentum)


def solution(mesh):
    placed = (
        P(("group", "shard"), None, None, None),
        P(("group", "shard"), None, None, None),
        P("group", "shard", None),
        P("group", "shard", None),
        P(),
    )
    return jax.shard_map(
        shards,
        mesh=mesh,
        in_specs=placed,
        out_specs=(
            P(("group", "shard"), None, None, None),
            P(("group", "shard"), None, None, None),
            P("group", "shard", None),
            P("group", "shard", None),
        ),
        check_vma=False,
    )
```

profile of v0, /device:TPU:32, one launch (start us, length us, event | category | flops | bytes accessed | tf_op | source)
XLA Modules:
  0.0 524.0 jit_solution(8767009696373970491)
XLA Ops:
  7.2 1.0 copy.38
  9.1 3.7 convolution_bitcast_fusion
  12.8 1.7 convolution_bitcast_fusion.1
  14.5 1.7 convolution_bitcast_fusion.2
  16.2 1.7 convolution_bitcast_fusion.3
  17.9 1.7 convolution_bitcast_fusion.5
  19.6 1.7 convolution_bitcast_fusion.6
  21.3 1.7 convolution_bitcast_fusion.7
  23.0 1.7 convolution_bitcast_fusion.8
  24.6 1.7 convolution_bitcast_fusion.4
  26.3 5.0 concatenate.3
  31.3 6.4 %pad_slice_fusion = (bf16[2,32,32,320]{3,2,1,0:T(8,128)(2,1)}, bf16[2,32,32,320]{3,2,1,0:T(8,128)(2,1)}, bf16[2,32,32,320]{3,2,1,0:T(8,128)(2,1)}, bf16[2,32,32,...) fusion(bf16[2,32,32,320]{3,2,1,0:T(8,128)(2,1)S(1)} %copy-done), kind=kLoop, calls=%fused_computation.16 | loop fusion | bytes 11796480 | tf_op jit(solution)/shard_map/slice | solution.py:22
  37.7 6.5 %pad_slice_fusion.8 = (bf16[2,32,32,320]{3,2,1,0:T(8,128)(2,1)}, bf16[2,32,32,320]{3,2,1,0:T(8,128)(2,1)}, bf16[2,32,32,320]{3,2,1,0:T(8,128)(2,1)}, bf16[2,32,3...) fusion(bf16[2,32,32,320]{3,2,1,0:T(8,128)(2,1)S(1)} %copy-done.2), kind=kLoop, calls=%fused_computation.24 | loop fusion | bytes 11796480 | tf_op jit(solution)/shard_map/slice | solution.py:22
  45.1 122.4 %all-gather.3.cloned.1.call-done = bf16[32,90,320]{2,1,0:T(8,128)(2,1)} async-done(((bf16[1,90,320]{2,1,0:T(8,128)(2,1)}), bf16[32,90,320]{2,1,0:T(8,128)(2,1)}) %all-gather.3.cloned.1.call-update) | async-done | bytes 1843216 | tf_op jit(solution)/shard_map/all_gather | solution.py:61
  167.5 2.9 reshape.109
  170.4 2.4 fusion.18
  172.8 0.9 convolution_add_fusion.7
  174.2 0.9 convolution_add_fusion.6
  175.6 0.9 convolution_add_fusion.5
  179.9 0.9 convolution_add_fusion.2
  181.3 0.9 convolution_add_fusion.1
  182.7 2.4 convolution_add_fusion
  185.1 3.4 copy.42
  188.5 2.4 fusion.16
  200.9 2.5 convolution_add_fusion.8
  203.3 3.5 copy.41
  206.8 290.9 %all-reduce.4.cloned.1.call-done = f32[2880,320]{0,1:T(8,128)} async-done(((f32[2880,320]{0,1:T(8,128)}), f32[2880,320]{0,1:T(8,128)}) %all-reduce.4.cloned.1.call-update) | async-done | bytes 3686416 | tf_op jit(solution)/shard_map/psum | solution.py:67
  497.7 1.1 bitcast_subtract_fusion
  498.8 16.8 %conditional.1 = (f32[90,320]{0,1:T(8,128)S(1)}, f32[90,320]{0,1:T(8,128)S(1)}) conditional(s32[]{:T(128)} %clamp.3, (f32[90,320]{0,1:T(8,128)S(1)}, f32[90,320]{0,1:T(8,128)S(1)}) %bitcast_subtract_fusion, (f32[90,320]{0,1:T(8,128)S(1)}, f32[90,320]{0,1:T(8,128)S(1)}) %bitcast_subtract_fusion, (f32[90,320]{0,1:T(8,128)S(1)}, ...), branch_computations={%region_1.2_spmd, %region_2.3_spmd, %region_3.4_spmd} | conditional | bytes 1843296 | solution.py:73
  499.0 5.6 %collective-permute-start.4 = (f32[90,320]{1,0:T(8,128)S(1)}, f32[90,320]{1,0:T(8,128)S(1)}, u32[]{:S(2)}, u32[]{:S(2)}) collective-permute-start(f32[90,320]{1,0:T(8,128)S(1)} %copy.48), channel_id=1, source_target_pairs={{0,128},{32,160},{64,192},{96,224},{128,0},{160,32},{192,64},{224,... | collective-permute-start | bytes 345608 | tf_op jit(solution)/shard_map/cond/branch_2_fun/ppermute | solution.py:16
  505.2 4.6 collective-permute-done.4
  510.0 5.5 %collective-permute-done.5 = f32[90,320]{1,0:T(8,128)S(1)} collective-permute-done((f32[90,320]{1,0:T(8,128)S(1)}, f32[90,320]{1,0:T(8,128)S(1)}, u32[]{:S(2)}, u32[]{:S(2)}) %collective-permute-start.5) | collective-permute-done | bytes 115232 | tf_op jit(solution)/shard_map/cond/branch_2_fun/ppermute | solution.py:16
  (62 shorter events, 18.7 us)
Async XLA Ops:
  7.2 160.3 %all-gather.3.cloned.1.call-start = ((), (), s32[]{:S(2)}) async-start(), calls=%async_computation.1 | async-start | bytes 2433024 | tf_op jit(solution)/shard_map/all_gather | solution.py:61
  9.0 3.8 copy-start
  9.1 3.8 copy-start.2
  9.1 488.7 %all-reduce.4.cloned.1.call-start = ((), (), s32[]{:S(2)}) async-start(), calls=%async_computation | async-start | bytes 7536640 | tf_op jit(solution)/shard_map/psum | solution.py:67
  37.7 7.2 %copy-start.18 = (f32[1,90,320]{2,0,1:T(1,128)S(1)}, f32[1,90,320]{2,0,1:T(1,128)}, u32[]{:S(2)}) copy-start(f32[1,90,320]{2,0,1:T(1,128)} %param.11) | copy-start | bytes 345604
  170.4 2.4 copy-start.17
  172.8 1.4 copy-start.16
  174.2 1.4 copy-start.15
  175.6 1.4 copy-start.1
  177.0 1.4 copy-start.14
  178.4 1.4 copy-start.13
  179.9 1.4 copy-start.12
  181.3 1.4 copy-start.11
  188.5 2.4 copy-start.10
  191.0 1.4 copy-start.9
  192.4 1.4 copy-start.8
  193.8 1.4 copy-start.3
  195.2 1.4 copy-start.7
  196.6 1.4 copy-start.6
  198.0 1.4 copy-start.5
  199.4 1.4 copy-start.4
  499.0 10.9 %collective-permute-start.4 = (f32[90,320]{1,0:T(8,128)S(1)}, f32[90,320]{1,0:T(8,128)S(1)}, u32[]{:S(2)}, u32[]{:S(2)}) collective-permute-start(f32[90,320]{1,0:T(8,128)S(1)} %copy.48), channel_id=1, source_target_pairs={{0,128},{32,160},{64,192},{96,224},{128,0},{160,32},{192,64},{224,... | collective-permute-start | bytes 345608 | tf_op jit(solution)/shard_map/cond/branch_2_fun/ppermute | solution.py:16
  504.7 10.7 %collective-permute-start.5 = (f32[90,320]{1,0:T(8,128)S(1)}, f32[90,320]{1,0:T(8,128)S(1)}, u32[]{:S(2)}, u32[]{:S(2)}) collective-permute-start(f32[90,320]{1,0:T(8,128)S(1)} %copy.49), channel_id=1, source_target_pairs={{0,128},{32,160},{64,192},{96,224},{128,0},{160,32},{192,64},{224,... | collective-permute-start | bytes 345608 | tf_op jit(solution)/shard_map/cond/branch_2_fun/ppermute | solution.py:16
Sparse Core Ops, SparseCore 0:
  10.3 157.0 all-gather.2
  170.1 327.5 all-reduce.3
where the time goes:
time: 525 us; the launch traced here: 524 us
  waiting for transfers between devices  423 us (81%)
  matrix products  39.5 us (8%)
  local copies, waits for them, and re-layouts  38.7 us (7%)
  between operations  15 us (3%)
  starting transfers between devices  6.17 us (1%)
    psum x1, waiting for transfers between devices, shards(): summed = lax.psum(partial_grad, 'shard')  291 us
    all_gather x1, waiting for transfers between devices, shards(): kernel = lax.all_gather(kernel_rows, 'shard', axis=0, tiled=True)  122 us
    dot_general x9, matrix products, conv_step(): lax.dot_general(moved_in, flat_co, (((0,), (0,)), ((), ())), preferred_el...  17.2 us
    unnamed x44, local copies, waits for them, and re-layouts  13.4 us
    slice x2, local copies, waits for them, and re-layouts, shifted_view(): padded[:, 1 + row_off:1 + row_off + height, 1 + col_off:1 + col_off + wid...  12.9 us
    dot_general x9, matrix products, conv_step(): jnp.dot(moved_in, tap_kernel, preferred_element_type=jnp.float32)  11.2 us
    dot_general x9, matrix products, conv_step(): lax.dot_general(moved_co, tap_kernel, (((1,), (1,)), ((), ())), preferred...  11.1 us
  transfers between devices with their start and end apart: 4, of which 4 were waited for; matrix products, arithmetic and copies ran while one was open for 13% of the time, Pallas kernels for 0%

commit v1 on v0

--- a/solution.py
+++ b/solution.py
@@ -58,7 +58,9 @@
 
 def shards(latents, cotangent, weights, momentum, step):
     kernel_rows = weights[0].astype(jnp.bfloat16)
-    kernel = lax.all_gather(kernel_rows, "shard", axis=0, tiled=True)
+    kernel = jnp.concatenate(
+        lax.all_to_all(jnp.stack([kernel_rows] * lax.axis_size("shard")), "shard", 0, 0), axis=0
+    )
     forward, backward, partial_grad = conv_step(latents, cotangent, kernel)
     cells_group = lax.axis_size("shard") * latents.shape[0] * latents.shape[1] * latents.shape[2]
     grad_scale = float(cells_group) ** (-0.5)

time: 525 us -> 393 us (0.75)
  waiting for transfers between devices: 423 us -> 285 us
  starting transfers between devices: 6.17 us -> 14.9 us
    all_gather x1 -> x0, waiting for transfers between devices: 122 us -> none  [shards(): kernel = lax.all_gather(kernel_rows, 'shard', axis=0, tiled=True)]
    psum x1, waiting for transfers between devices: 291 us -> 275 us  [shards(): summed = lax.psum(partial_grad, 'shard')]
    all_to_all x0 -> x1, starting transfers between devices: none -> 8.73 us  [shards(): lax.all_to_all(jnp.stack([kernel_rows] * lax.axis_size('shard')), 'shard'...]
    unnamed x44 -> x47, local copies, waits for them, and re-layouts: 13.4 us -> 9.08 us
  transfers between devices with their start and end apart: 4 -> 4, of which waited for: 4 -> 3; matrix products, arithmetic and copies ran while one was open for 13% -> 16% of each run, Pallas kernels for 0% -> 0%
where the time goes in v1:
time: 393 us; the launch traced here: 392 us
  waiting for transfers between devices  285 us (73%)
  local copies, waits for them, and re-layouts  38.6 us (10%)
  matrix products  36.7 us (9%)
  between operations  15.1 us (4%)
  starting transfers between devices  14.9 us (4%)
    psum x1, waiting for transfers between devices, shards(): summed = lax.psum(partial_grad, 'shard')  275 us
    dot_general x9, matrix products, conv_step(): lax.dot_general(moved_in, flat_co, (((0,), (0,)), ((), ())), preferred_el...  14.4 us
    slice x2, local copies, waits for them, and re-layouts, shifted_view(): padded[:, 1 + row_off:1 + row_off + height, 1 + col_off:1 + col_off + wid...  12.9 us
    dot_general x9, matrix products, conv_step(): jnp.dot(moved_in, tap_kernel, preferred_element_type=jnp.float32)  11.2 us
    dot_general x9, matrix products, conv_step(): lax.dot_general(moved_co, tap_kernel, (((1,), (1,)), ((), ())), preferred...  11.1 us
    ppermute x2, waiting for transfers between devices, from_partner(): return lax.ppermute(value, axis, pairs)  10.1 us
    unnamed x47, local copies, waits for them, and re-layouts  9.08 us
    all_to_all x1, starting transfers between devices, shards(): lax.all_to_all(jnp.stack([kernel_rows] * lax.axis_size('shard')), 'shard'...  8.73 us
  transfers between devices with their start and end apart: 4, of which 3 were waited for; matrix products, arithmetic and copies ran while one was open for 16% of the time, Pallas kernels for 0%

profile of v1, /device:TPU:32, one launch (start us, length us, event | category | flops | bytes accessed | tf_op | source)
XLA Modules:
  0.0 392.1 jit_solution(2774440474400075464)
XLA Ops:
  7.2 1.0 convert_element_type.11
  8.2 1.6 stack.5
  9.8 8.7 %all-to-all-start = ((bf16[32,90,320]{2,1,0:T(8,128)(2,1)}), bf16[32,90,320]{2,1,0:T(8,128)(2,1)}, u32[]{:S(2)}, u32[]{:S(2)}) async-start(bf16[32,90,320]{2,1,0:T(8,128)(2,1)} %stack.5), calls=%async_computation | async-start | bytes 4718592 | tf_op jit(solution)/shard_map/all_to_all | solution.py:62
  18.6 2.4 convolution_bitcast_fusion
  22.8 1.7 convolution_bitcast_fusion.3
  24.5 1.7 convolution_bitcast_fusion.5
  26.3 1.7 convolution_bitcast_fusion.6
  28.0 1.7 convolution_bitcast_fusion.7
  29.7 1.7 convolution_bitcast_fusion.8
  31.3 1.7 convolution_bitcast_fusion.4
  33.0 4.7 %concatenate.3 = f32[2880,320]{0,1:T(8,128)} concatenate(f32[320,320]{0,1:T(8,128)} %convolution_bitcast_fusion.8, f32[320,320]{0,1:T(8,128)} %convolution_bitcast_fusion.7, f32[320,320]{0,1:T(8,128)} %convolution_bitcast_fusion.6, f32[320,320]{0,1:T(8,128)} %convolution_bitcast_fusion.5, f32[320,320]{0,1:T(8,128)} %convolution_bitcast_fusion.4, ...), dimensions={0} | concatenate | bytes 7372800 | tf_op jit(solution)/shard_map/concatenate | solution.py:51
  39.0 6.4 %pad_slice_fusion = (bf16[2,32,32,320]{3,2,1,0:T(8,128)(2,1)}, bf16[2,32,32,320]{3,2,1,0:T(8,128)(2,1)}, bf16[2,32,32,320]{3,2,1,0:T(8,128)(2,1)}, bf16[2,32,32,...) fusion(bf16[2,32,32,320]{3,2,1,0:T(8,128)(2,1)S(1)} %copy-done), kind=kLoop, calls=%fused_computation.16 | loop fusion | bytes 11796480 | tf_op jit(solution)/shard_map/slice | solution.py:22
  45.4 6.5 %pad_slice_fusion.8 = (bf16[2,32,32,320]{3,2,1,0:T(8,128)(2,1)}, bf16[2,32,32,320]{3,2,1,0:T(8,128)(2,1)}, bf16[2,32,32,320]{3,2,1,0:T(8,128)(2,1)}, bf16[2,32,3...) fusion(bf16[2,32,32,320]{3,2,1,0:T(8,128)(2,1)S(1)} %copy-done.3), kind=kLoop, calls=%fused_computation.24 | loop fusion | bytes 11796480 | tf_op jit(solution)/shard_map/slice | solution.py:22
  51.9 2.9 reshape.112
  54.8 2.4 fusion.18
  57.3 0.9 convolution_add_fusion.7
  58.7 0.9 convolution_add_fusion.6
  61.5 0.9 convolution_add_fusion.4
  62.9 0.9 convolution_add_fusion.3
  64.3 0.9 convolution_add_fusion.2
  65.7 0.9 convolution_add_fusion.1
  67.1 2.4 convolution_add_fusion
  69.5 3.4 copy.40
  73.0 2.4 fusion.16
  85.3 2.5 convolution_add_fusion.8
  87.8 3.5 copy.39
  91.3 274.5 %all-reduce.4.cloned.1.call-done = f32[2880,320]{0,1:T(8,128)} async-done(((f32[2880,320]{0,1:T(8,128)}), f32[2880,320]{0,1:T(8,128)}) %all-reduce.4.cloned.1.call-update) | async-done | bytes 3686416 | tf_op jit(solution)/shard_map/psum | solution.py:69
  365.8 1.1 bitcast_subtract_fusion
  366.9 16.8 %conditional.1 = (f32[90,320]{0,1:T(8,128)S(1)}, f32[90,320]{0,1:T(8,128)S(1)}) conditional(s32[]{:T(128)} %clamp.3, (f32[90,320]{0,1:T(8,128)S(1)}, f32[90,320]{0,1:T(8,128)S(1)}) %bitcast_subtract_fusion, (f32[90,320]{0,1:T(8,128)S(1)}, f32[90,320]{0,1:T(8,128)S(1)}) %bitcast_subtract_fusion, (f32[90,320]{0,1:T(8,128)S(1)}, ...), branch_computations={%region_1.2_spmd, %region_2.3_spmd, %region_3.4_spmd} | conditional | bytes 1843296 | solution.py:75
  367.1 5.6 %collective-permute-start.4 = (f32[90,320]{1,0:T(8,128)S(1)}, f32[90,320]{1,0:T(8,128)S(1)}, u32[]{:S(2)}, u32[]{:S(2)}) collective-permute-start(f32[90,320]{1,0:T(8,128)S(1)} %copy.47), channel_id=1, source_target_pairs={{0,128},{32,160},{64,192},{96,224},{128,0},{160,32},{192,64},{224,... | collective-permute-start | bytes 345608 | tf_op jit(solution)/shard_map/cond/branch_2_fun/ppermute | solution.py:16
  373.3 4.6 %collective-permute-done.4 = f32[90,320]{1,0:T(8,128)S(1)} collective-permute-done((f32[90,320]{1,0:T(8,128)S(1)}, f32[90,320]{1,0:T(8,128)S(1)}, u32[]{:S(2)}, u32[]{:S(2)}) %collective-permute-start.4) | collective-permute-done | bytes 115232 | tf_op jit(solution)/shard_map/cond/branch_2_fun/ppermute | solution.py:16
  378.0 5.5 %collective-permute-done.5 = f32[90,320]{1,0:T(8,128)S(1)} collective-permute-done((f32[90,320]{1,0:T(8,128)S(1)}, f32[90,320]{1,0:T(8,128)S(1)}, u32[]{:S(2)}, u32[]{:S(2)}) %collective-permute-start.5) | collective-permute-done | bytes 115232 | tf_op jit(solution)/shard_map/cond/branch_2_fun/ppermute | solution.py:16
  (66 shorter events, 19.2 us)
Async XLA Ops:
  9.8 8.8 %copy-start = (bf16[2,32,32,320]{3,2,1,0:T(8,128)(2,1)S(1)}, bf16[2,32,32,320]{3,2,1,0:T(8,128)(2,1)}, u32[]{:S(2)}) copy-start(bf16[2,32,32,320]{3,2,1,0:T(8,128)(2,1)} %param.9) | copy-start | bytes 3932164
  9.8 42.1 %all-to-all-start = ((bf16[32,90,320]{2,1,0:T(8,128)(2,1)}), bf16[32,90,320]{2,1,0:T(8,128)(2,1)}, u32[]{:S(2)}, u32[]{:S(2)}) async-start(bf16[32,90,320]{2,1,0:T(8,128)(2,1)} %stack.5), calls=%async_computation | async-start | bytes 4718592 | tf_op jit(solution)/shard_map/all_to_all | solution.py:62
  18.5 347.3 %all-reduce.4.cloned.1.call-start = ((), (), s32[]{:S(2)}) async-start(), calls=%async_computation.1 | async-start | bytes 7536640 | tf_op jit(solution)/shard_map/psum | solution.py:69
  18.6 2.4 copy-start.2
  37.7 0.9 copy-start.19
  37.7 1.1 copy-start.20
  39.0 6.4 %copy-start.3 = (bf16[2,32,32,320]{3,2,1,0:T(8,128)(2,1)S(1)}, bf16[2,32,32,320]{3,2,1,0:T(8,128)(2,1)}, u32[]{:S(2)}) copy-start(bf16[2,32,32,320]{3,2,1,0:T(8,128)(2,1)} %param.8) | copy-start | bytes 3932164
  54.8 2.4 copy-start.18
  57.2 1.4 copy-start.17
  58.7 1.4 copy-start.16
  60.1 1.4 copy-start.1
  61.5 1.4 copy-start.15
  62.9 1.4 copy-start.14
  64.3 1.4 copy-start.13
  65.7 1.4 copy-start.12
  73.0 2.4 copy-start.11
  75.4 1.4 copy-start.10
  76.8 1.4 copy-start.9
  78.2 1.4 copy-start.4
  79.7 1.4 copy-start.8
  81.1 1.4 copy-start.7
  82.5 1.4 copy-start.6
  83.9 1.4 copy-start.5
  367.1 10.9 %collective-permute-start.4 = (f32[90,320]{1,0:T(8,128)S(1)}, f32[90,320]{1,0:T(8,128)S(1)}, u32[]{:S(2)}, u32[]{:S(2)}) collective-permute-start(f32[90,320]{1,0:T(8,128)S(1)} %copy.47), channel_id=1, source_target_pairs={{0,128},{32,160},{64,192},{96,224},{128,0},{160,32},{192,64},{224,... | collective-permute-start | bytes 345608 | tf_op jit(solution)/shard_map/cond/branch_2_fun/ppermute | solution.py:16
  372.8 10.7 %collective-permute-start.5 = (f32[90,320]{1,0:T(8,128)S(1)}, f32[90,320]{1,0:T(8,128)S(1)}, u32[]{:S(2)}, u32[]{:S(2)}) collective-permute-start(f32[90,320]{1,0:T(8,128)S(1)} %copy.48), channel_id=1, source_target_pairs={{0,128},{32,160},{64,192},{96,224},{128,0},{160,32},{192,64},{224,... | collective-permute-start | bytes 345608 | tf_op jit(solution)/shard_map/cond/branch_2_fun/ppermute | solution.py:16
Sparse Core Ops, SparseCore 0:
  37.9 327.8 all-reduce.3
